TPU v7x, 512 devices: a whole 4x8x8 slice. The times are simulated.
512 devices in a mesh: row: 16 (over y, core), col: 32 (over z, x).
Axes of the slice: x: 4, y: 8, z: 8, core: 2. Of those that a mesh axis runs over, the one named last changes fastest.
Arguments:
- points: bfloat16 [128, 65536], P(None, ('row', 'col')), may hold values from -6 to 6
- inv_scale: float32 [128], replicated, may hold values from 0.07 to 0.22
- basis: bfloat16 [65536, 4096], P(('row', 'col')), may hold values from -0.25 to 0.25
- shrink: float32 [4096], replicated, may hold values from 0.02 to 1
- solution: float32 [33, 65536], P(None, ('row', 'col')), may hold values from -6 to 6
- residual: float32 [33, 65536], P(None, ('row', 'col')), may hold values from -6 to 6
- direction_prev: float32 [33, 65536], P(None, ('row', 'col')), may hold values from -6 to 6
- rz_prev: float32 [33], replicated, may hold values from 65536 to 262144
Outputs:
- solution_next: float32 [33, 65536], P(None, ('row', 'col'))
- residual_next: float32 [33, 65536], P(None, ('row', 'col'))
- direction: float32 [33, 65536], P(None, ('row', 'col'))
All inputs are finite; a program needn't handle non-finite values.
Results may differ from a plain program's by a relative error of at most 0.019.
Values may be sent and summed in bfloat16 or wider, within the bound.
A program may use at most 64 MiB of HBM per device.

v0:
```python
import jax
import jax.numpy as jnp
from jax import lax
from jax.sharding import PartitionSpec as P

noise_level = 0.25


def local(points, inv_scale, basis, shrink, solution, residual, direction_prev, rz_prev):
    scaled = (points * inv_scale[:, None]).astype(jnp.bfloat16)
    residual_bf = residual.astype(jnp.bfloat16)
    local_proj = jnp.dot(residual_bf, basis, preferred_element_type=jnp.float32)
    damping = shrink - 1.0
    projected = lax.psum(local_proj, ("row", "col"))
    correction = (damping[None, :] * projected).astype(jnp.bfloat16)
    precond = residual + jnp.dot(correction, basis.T, preferred_element_type=jnp.float32)
    precond_inner = lax.psum(jnp.sum(residual * precond, axis=1), ("row", "col"))
    direction = precond + (precond_inner / rz_prev)[:, None] * direction_prev
    direction_bf = direction.astype(jnp.bfloat16)
    row_points = lax.all_gather(scaled, "col", axis=1, tiled=True)
    row_sq = jnp.sum(jnp.square(row_points.astype(jnp.float32)), axis=0)
    rows_total = row_points.shape[1]
    width = min(1024, rows_total)
    direction_piece = lax.all_gather(direction_bf, "row", axis=1, tiled=True)
    column_pts = lax.all_gather(scaled, "row", axis=1, tiled=True)
    column_sq = jnp.sum(jnp.square(column_pts.astype(jnp.float32)), axis=0)
    results = []
    for offset in range(0, rows_total, width):
        rows = row_points[:, offset : offset + width]
        cross = lax.dot_general(
            column_pts, rows, (((0,), (0,)), ((), ())), preferred_element_type=jnp.float32
        )
        distance = jnp.maximum(
            column_sq[:, None] + row_sq[None, offset : offset + width] - 2.0 * cross, 0.0
        )
        tile = jnp.exp(-0.5 * distance).astype(jnp.bfloat16)
        results.append(jnp.dot(direction_piece, tile, preferred_element_type=jnp.float32))
    image_part = jnp.concatenate(results, axis=1)
    image = (
        lax.psum_scatter(
            image_part.astype(jnp.bfloat16), "col", scatter_dimension=1, tiled=True
        ).astype(jnp.float32)
        + noise_level * direction
    )
    curvature = lax.psum(jnp.sum(direction * image, axis=1), ("row", "col"))
    alpha = precond_inner / curvature
    solution_next = solution + alpha[:, None] * direction
    residual_next = residual - alpha[:, None] * image
    return (solution_next, residual_next, direction)


def solution(mesh):
    placed = (
        P(None, ("row", "col")),
        P(),
        P(("row", "col"), None),
        P(),
        P(None, ("row", "col")),
        P(None, ("row", "col")),
        P(None, ("row", "col")),
        P(),
    )
    return jax.shard_map(
        local,
        mesh=mesh,
        in_specs=placed,
        out_specs=(P(None, ("row", "col")), P(None, ("row", "col")), P(None, ("row", "col"))),
        check_vma=False,
    )
```

profile of v0, /device:TPU:1, one launch (start us, length us, event | category | flops | bytes accessed | tf_op | source)
XLA Modules:
  0.0 740.1 jit_solution(11344339179035116326)
XLA Ops:
  8.0 0.0 copy-start
  8.0 0.0 copy-start.4
  8.0 0.0 copy-start.8
  8.0 0.0 all-reduce.2.cloned.1.call-start
  8.1 1.2 copy-done
  9.2 1.9 fusion.17
  11.1 0.0 all-reduce.2.cloned.1.call-update
  11.1 0.0 all-gather.2.cloned.1.call-start
  11.2 0.0 copy-done.4
  11.2 0.7 multiply_convert_fusion.2
  11.9 0.0 all-gather.2.cloned.1.call-update
  11.9 0.0 reduce-scatter.4.cloned.1.call-start
  11.9 22.7 %all_gather.10 = bf16[128,2048]{1,0:T(8,128)(2,1)S(1)} all-gather(bf16[128,128]{1,0:T(8,128)(2,1)} %multiply_convert_fusion.2), channel_id=1, replica_groups=mesh['row'=16,'col'=32] {'row'}, dimensions={1}, use_global_device_ids=true | all-gather | bytes 557056 | tf_op jit(solution)/shard_map/all_gather | solution.py:25
  34.6 0.1 multiply_reduce_fusion.1
  34.8 256.8 %all-reduce.2.cloned.1.call-done = f32[33,4096]{1,0:T(8,128)} async-done(((f32[33,4096]{1,0:T(8,128)}), f32[33,4096]{1,0:T(8,128)}) %all-reduce.2.cloned.1.call-update) | async-done | bytes 540688 | tf_op jit(solution)/shard_map/psum | solution.py:14
  291.6 1.7 multiply_reduce_fusion.3
  293.3 97.0 %psum.22 = f32[33]{0:T(128)S(1)} all-reduce(f32[33]{0:T(128)S(1)} %get-tuple-element.11), channel_id=1, replica_groups=mesh['row'=16,'col'=32] {'row','col'}, use_global_device_ids=true, to_apply=%region_2.0 | all-reduce | flops 33 | bytes 264 | tf_op jit(solution)/shard_map/psum | solution.py:17
  390.3 0.1 fusion.31
  390.4 15.4 %all_gather.9 = bf16[33,2048]{1,0:T(8,128)(2,1)S(1)} all-gather(bf16[33,128]{1,0:T(8,128)(2,1)S(1)} %get-tuple-element.3), channel_id=1, replica_groups=mesh['row'=16,'col'=32] {'row'}, dimensions={1}, use_global_device_ids=true | all-gather | bytes 143616 | tf_op jit(solution)/shard_map/all_gather | solution.py:24
  405.7 1.5 multiply_reduce_fusion
  407.3 2.7 fusion.4
  410.0 2.7 fusion.5
  412.7 2.7 fusion.6
  415.5 2.7 fusion.7
  418.2 0.0 copy-start.5
  418.2 1.4 copy.11
  419.6 0.0 reduce-scatter.4.cloned.1.call-update
  419.7 210.6 %reduce-scatter.4.cloned.1.call-done = bf16[128,33]{1,0:T(8,128)(2,1)} async-done(((bf16[4096,33]{1,0:T(8,128)(2,1)}), bf16[128,33]{1,0:T(8,128)(2,1)}) %reduce-scatter.4.cloned.1.call-update) | async-done | bytes 8464
  630.3 0.8 copy.12
  631.1 0.1 multiply_reduce_fusion.2
  631.2 100.7 %psum.23 = f32[33]{0:T(128)S(1)} all-reduce(f32[33]{0:T(128)S(1)} %multiply_reduce_fusion.2), channel_id=1, replica_groups=mesh['row'=16,'col'=32] {'row','col'}, use_global_device_ids=true, to_apply=%region_7.0 | all-reduce | flops 33 | bytes 264 | tf_op jit(solution)/shard_map/psum | solution.py:45
  731.9 0.7 multiply_subtract_fusion
  (20 shorter events, 0.1 us)
Async XLA Ops:
  8.0 1.2 copy-start
  8.0 3.2 copy-start.4
  8.0 3.2 copy-start.8
  8.0 283.6 %all-reduce.2.cloned.1.call-start = ((), (), s32[]{:S(2)}) async-start(), calls=%async_computation.1 | async-start | bytes 1310720 | tf_op jit(solution)/shard_map/psum | solution.py:14
  11.1 23.7 %copy-start.7 = (f32[4096]{0:T(1024)S(1)}, f32[4096]{0:T(1024)}, u32[]{:S(2)}) copy-start(f32[4096]{0:T(1024)} %param.11) | copy-start | bytes 49156
  11.1 280.5 %copy-start.3 = (f32[33,128]{1,0:T(8,128)S(1)}, f32[33,128]{1,0:T(8,128)}, u32[]{:S(2)}) copy-start(f32[33,128]{1,0:T(8,128)} %param.13) | copy-start | bytes 50692
  11.1 394.6 %all-gather.2.cloned.1.call-start = ((), (), s32[]{:S(2)}) async-start(), calls=%async_computation.2 | async-start | bytes 1081344 | tf_op jit(solution)/shard_map/all_gather | solution.py:20
  11.9 618.4 %reduce-scatter.4.cloned.1.call-start = ((), (), s32[]{:S(2)}) async-start(), calls=%async_computation.3 | async-start | bytes 1081344
  34.6 355.6 %copy-start.9 = (f32[33]{0:T(128)S(1)}, f32[33]{0:T(128)}, u32[]{:S(2)}) copy-start(f32[33]{0:T(128)} %param.15) | copy-start | bytes 400
  34.6 355.6 %copy-start.6 = (f32[33,128]{1,0:T(8,128)S(1)}, f32[33,128]{1,0:T(8,128)}, u32[]{:S(2)}) copy-start(f32[33,128]{1,0:T(8,128)} %param.14) | copy-start | bytes 50692
  390.4 341.6 %copy-start.2 = (f32[33,128]{1,0:T(8,128)}, f32[33,128]{1,0:T(8,128)S(1)}, u32[]{:S(2)}) copy-start(f32[33,128]{1,0:T(8,128)S(1)} %get-tuple-element.4) | copy-start | bytes 50692
  405.7 1.6 copy-start.1
  418.2 313.7 %copy-start.5 = (f32[33,128]{1,0:T(8,128)S(1)}, f32[33,128]{1,0:T(8,128)}, u32[]{:S(2)}) copy-start(f32[33,128]{1,0:T(8,128)} %param.12) | copy-start | bytes 50692
Sparse Core Ops, SparseCore 0:
  13.8 277.7 all-reduce.1
Sparse Core Ops, SparseCore 1:
  15.1 78.6 all-gather.1
  419.7 210.5 reduce-scatter.3
where the time goes:
time: 740 us
  waiting for transfers between devices  467 us (63%)
  blocking collectives  236 us (32%)
  between operations  15.6 us (2%)
  matrix products  14.4 us (2%)
    psum x1, waiting for transfers between devices, local(): projected = lax.psum(local_proj, ('row', 'col'))  257 us
    unnamed x4, waiting for transfers between devices  211 us
    psum x1, blocking collectives, local(): curvature = lax.psum(jnp.sum(direction * image, axis=1), ('row', 'col'))  101 us
    psum x1, blocking collectives, local(): lax.psum(jnp.sum(residual * precond, axis=1), ('row', 'col'))  97 us
    all_gather x1, blocking collectives, local(): column_pts = lax.all_gather(scaled, 'row', axis=1, tiled=True)  22.7 us
    all_gather x1, blocking collectives, local(): direction_piece = lax.all_gather(direction_bf, 'row', axis=1, tiled=True)  15.4 us
  transfers between devices with their start and end apart: 3, of which 2 were waited for; matrix products, arithmetic and copies ran while one was open for 0% of the time, Pallas kernels for 0%

commit v1 on v0

--- a/solution.py
+++ b/solution.py
@@ -4,6 +4,13 @@
 from jax.sharding import PartitionSpec as P
 
 noise_level = 0.25
+
+
+def trace_view_on(work_x):
+    r1 = lax.axis_size("row")
+    mid_arr = jnp.stack([work_x] * r1, axis=0)
+    formed = lax.all_to_all(mid_arr, "row", 0, 0)
+    return jnp.concatenate(formed, axis=1)
 
 
 def local(points, inv_scale, basis, shrink, solution, residual, direction_prev, rz_prev):
@@ -22,7 +29,7 @@
     rows_total = row_points.shape[1]
     width = min(1024, rows_total)
     direction_piece = lax.all_gather(direction_bf, "row", axis=1, tiled=True)
-    column_pts = lax.all_gather(scaled, "row", axis=1, tiled=True)
+    column_pts = trace_view_on(scaled)
     column_sq = jnp.sum(jnp.square(column_pts.astype(jnp.float32)), axis=0)
     results = []
     for offset in range(0, rows_total, width):

time: 740 us -> 741 us (level)
  blocking collectives: 236 us -> 213 us
  waiting for transfers between devices: 467 us -> 479 us
  starting transfers between devices: 0.13 us -> 10.4 us
    all_gather x1 -> x0, blocking collectives: 22.7 us -> none  [local(): column_pts = lax.all_gather(scaled, 'row', axis=1, tiled=True)]
    psum x1, waiting for transfers between devices: 257 us -> 268 us  [local(): projected = lax.psum(local_proj, ('row', 'col'))]
    all_to_all x0 -> x1, starting transfers between devices: none -> 10.2 us  [trace_view_on(): formed = lax.all_to_all(mid_arr, 'row', 0, 0)]
  transfers between devices with their start and end apart: 3 -> 4, of which waited for: 2 -> 2; matrix products, arithmetic and copies ran while one was open for 0% -> 1% of each run, Pallas kernels for 0% -> 0%
where the time goes in v1:
time: 741 us
  waiting for transfers between devices  479 us (65%)
  blocking collectives  213 us (29%)
  between operations  15.7 us (2%)
  matrix products  13.8 us (2%)
  starting transfers between devices  10.4 us (1%)
    psum x1, waiting for transfers between devices, local(): projected = lax.psum(local_proj, ('row', 'col'))  268 us
    unnamed x4, waiting for transfers between devices  211 us
    psum x1, blocking collectives, local(): curvature = lax.psum(jnp.sum(direction * image, axis=1), ('row', 'col'))  101 us
    psum x1, blocking collectives, local(): lax.psum(jnp.sum(residual * precond, axis=1), ('row', 'col'))  97 us
    all_gather x1, blocking collectives, local(): direction_piece = lax.all_gather(direction_bf, 'row', axis=1, tiled=True)  15.4 us
  transfers between devices with their start and end apart: 4, of which 2 were waited for; matrix products, arithmetic and copies ran while one was open for 1% of the time, Pallas kernels for 0%

profile of v1, /device:TPU:1, one launch (start us, length us, event | category | flops | bytes accessed | tf_op | source)
XLA Modules:
  0.0 740.9 jit_solution(16758987094460423741)
XLA Ops:
  8.0 0.0 copy-start
  8.0 0.0 all-reduce.2.cloned.1.call-start
  8.1 1.2 copy-done
  9.2 1.9 fusion.17
  11.1 0.0 all-reduce.2.cloned.1.call-update
  11.1 0.0 copy-start.7
  11.1 0.0 all-gather.2.cloned.1.call-start
  11.2 0.7 multiply_convert_fusion.2
  11.9 0.0 all-gather.2.cloned.1.call-update
  11.9 0.9 copy.12
  12.8 0.9 stack.2
  13.7 10.2 %all-to-all-start = ((bf16[16,128,128]{1,2,0:T(8,128)(2,1)}), bf16[16,128,128]{1,2,0:T(8,128)(2,1)S(1)}, u32[]{:S(2)}, u32[]{:S(2)}) async-start(bf16[16,128,128]{1,2,0:T(8,128)(2,1)} %stack.2), calls=%async_computation | async-start | bytes 1048576 | tf_op jit(solution)/shard_map/all_to_all | solution.py:12
  24.0 0.0 reduce-scatter.4.cloned.1.call-start
  24.1 268.2 %all-reduce.2.cloned.1.call-done = f32[33,4096]{1,0:T(8,128)} async-done(((f32[33,4096]{1,0:T(8,128)}), f32[33,4096]{1,0:T(8,128)}) %all-reduce.2.cloned.1.call-update) | async-done | bytes 540688 | tf_op jit(solution)/shard_map/psum | solution.py:21
  292.2 1.7 multiply_reduce_fusion.3
  293.9 97.0 %psum.22 = f32[33]{0:T(128)S(1)} all-reduce(f32[33]{0:T(128)S(1)} %get-tuple-element.11), channel_id=1, replica_groups=mesh['row'=16,'col'=32] {'row','col'}, use_global_device_ids=true, to_apply=%region_2.0 | all-reduce | flops 33 | bytes 264 | tf_op jit(solution)/shard_map/psum | solution.py:24
  390.9 0.1 fusion.31
  391.0 15.4 %all_gather.6 = bf16[33,2048]{1,0:T(8,128)(2,1)S(1)} all-gather(bf16[33,128]{1,0:T(8,128)(2,1)S(1)} %get-tuple-element.3), channel_id=1, replica_groups=mesh['row'=16,'col'=32] {'row'}, dimensions={1}, use_global_device_ids=true | all-gather | bytes 143616 | tf_op jit(solution)/shard_map/all_gather | solution.py:31
  406.3 0.3 multiply_reduce_fusion.1
  406.7 0.0 all-gather.2.cloned.1.call-done
  406.7 1.5 multiply_reduce_fusion
  408.3 2.6 fusion.4
  410.9 2.6 fusion.5
  413.4 2.6 fusion.6
  416.0 2.6 fusion.7
  418.6 1.4 copy.13
  420.0 0.0 reduce-scatter.4.cloned.1.call-update
  420.0 211.0 %reduce-scatter.4.cloned.1.call-done = bf16[128,33]{1,0:T(8,128)(2,1)} async-done(((bf16[4096,33]{1,0:T(8,128)(2,1)}), bf16[128,33]{1,0:T(8,128)(2,1)}) %reduce-scatter.4.cloned.1.call-update) | async-done | bytes 8464
  631.0 0.8 copy.14
  631.9 0.1 multiply_reduce_fusion.2
  632.0 100.7 %psum.23 = f32[33]{0:T(128)S(1)} all-reduce(f32[33]{0:T(128)S(1)} %multiply_reduce_fusion.2), channel_id=1, replica_groups=mesh['row'=16,'col'=32] {'row','col'}, use_global_device_ids=true, to_apply=%region_7.0 | all-reduce | flops 33 | bytes 264 | tf_op jit(solution)/shard_map/psum | solution.py:52
  732.7 0.7 multiply_subtract_fusion
  (23 shorter events, 0.1 us)
Async XLA Ops:
  8.0 1.2 copy-start
  8.0 3.2 copy-start.4
  8.0 3.2 copy-start.8
  8.0 284.2 %all-reduce.2.cloned.1.call-start = ((), (), s32[]{:S(2)}) async-start(), calls=%async_computation.2 | async-start | bytes 1310720 | tf_op jit(solution)/shard_map/psum | solution.py:21
  11.1 12.9 %copy-start.7 = (f32[4096]{0:T(1024)S(1)}, f32[4096]{0:T(1024)}, u32[]{:S(2)}) copy-start(f32[4096]{0:T(1024)} %param.11) | copy-start | bytes 49156
  11.1 281.1 %copy-start.3 = (f32[33,128]{1,0:T(8,128)S(1)}, f32[33,128]{1,0:T(8,128)}, u32[]{:S(2)}) copy-start(f32[33,128]{1,0:T(8,128)} %param.13) | copy-start | bytes 50692
  11.1 395.6 %all-gather.2.cloned.1.call-start = ((), (), s32[]{:S(2)}) async-start(), calls=%async_computation.3 | async-start | bytes 1081344 | tf_op jit(solution)/shard_map/all_gather | solution.py:27
  13.7 392.6 %all-to-all-start = ((bf16[16,128,128]{1,2,0:T(8,128)(2,1)}), bf16[16,128,128]{1,2,0:T(8,128)(2,1)S(1)}, u32[]{:S(2)}, u32[]{:S(2)}) async-start(bf16[16,128,128]{1,2,0:T(8,128)(2,1)} %stack.2), calls=%async_computation | async-start | bytes 1048576 | tf_op jit(solution)/shard_map/all_to_all | solution.py:12
  24.0 366.9 %copy-start.9 = (f32[33]{0:T(128)S(1)}, f32[33]{0:T(128)}, u32[]{:S(2)}) copy-start(f32[33]{0:T(128)} %param.15) | copy-start | bytes 400
  24.0 366.9 %copy-start.6 = (f32[33,128]{1,0:T(8,128)S(1)}, f32[33,128]{1,0:T(8,128)}, u32[]{:S(2)}) copy-start(f32[33,128]{1,0:T(8,128)} %param.14) | copy-start | bytes 50692
  24.0 607.1 %reduce-scatter.4.cloned.1.call-start = ((), (), s32[]{:S(2)}) async-start(), calls=%async_computation.4 | async-start | bytes 1081344
  391.0 341.7 %copy-start.2 = (f32[33,128]{1,0:T(8,128)}, f32[33,128]{1,0:T(8,128)S(1)}, u32[]{:S(2)}) copy-start(f32[33,128]{1,0:T(8,128)S(1)} %get-tuple-element.4) | copy-start | bytes 50692
  406.7 1.6 copy-start.1
  418.6 314.1 %copy-start.5 = (f32[33,128]{1,0:T(8,128)S(1)}, f32[33,128]{1,0:T(8,128)}, u32[]{:S(2)}) copy-start(f32[33,128]{1,0:T(8,128)} %param.12) | copy-start | bytes 50692
Sparse Core Ops, SparseCore 0:
  13.8 278.3 all-reduce.1
Sparse Core Ops, SparseCore 1:
  15.1 78.7 all-gather.1
  420.1 210.9 reduce-scatter.3
